TPU v7x, 32 devices: a whole 2x2x4 slice. The times are simulated.
32 devices in a mesh: parts: 2 (over x), seq: 16 (over z, y, core).
Axes of the slice: x: 2, y: 2, z: 4, core: 2. Of those that a mesh axis runs over, the one named last changes fastest.
Arguments:
- prefix_latent: bfloat16 [61440, 512], P(('parts', 'seq')), parts along dimension 0, may hold values from -6 to 6
- block_order: int32 [480], P(('parts', 'seq')), parts along dimension 0, may hold values from 0 to 239, each once
- key_up: bfloat16 [512, 512], replicated, may hold values from -0.25 to 0.25
- value_up: bfloat16 [512, 512], replicated, may hold values from -0.25 to 0.25
- queries: bfloat16 [32, 4, 4096], P(('parts', 'seq')), parts along dimension 0, may hold values from -200 to 200
- new_keys: bfloat16 [32, 4, 512], P(('parts', 'seq')), parts along dimension 0, may hold values from -6 to 6
- new_values: bfloat16 [32, 4, 512], P(('parts', 'seq')), parts along dimension 0, may hold values from -6 to 6
- suffix_keys: bfloat16 [32, 4096, 512], P(('parts', 'seq')), parts along dimension 0, may hold values from -6 to 6
- suffix_values: bfloat16 [32, 4096, 512], P(('parts', 'seq')), parts along dimension 0, may hold values from -6 to 6
- suffix_len: int32 [32], P(('parts', 'seq')), parts along dimension 0, may hold values from 1 to 4096, 32768 in all
Outputs:
- attended: bfloat16 [32, 4, 4096], P(('parts', 'seq')), parts along dimension 0
There are 2 independent parts, one for each index of `parts`. A program takes and returns all parts, laid end to end along the dimension named above; an argument that names none is the same for every part. Nothing has to cross between parts.
Inputs may be any that keep to these rules, and one draw needn't show every extreme that they name: A request's cache holds its first suffix_len entries; some request holds exactly 4096. `block_order`: each block position appears once.
All inputs are finite; a program needn't handle non-finite values. No bound on the sum of `suffix_len` on one device may be relied on, other than what follows from the above.
Results may differ from a plain program's by a relative error of at most 0.005.
The roundings to bfloat16 on the way count: a program that leaves them out, or rounds other values in their place, can miss the bound.
Values may be sent and summed in bfloat16 or wider, within the bound.
No kernel may reach another device: no remote copies, remote signals or barrier semaphores. Data moves between devices by JAX's collectives and lax.ppermute only.
A program may use at most 128 MiB of HBM per device.

v0:
```python
import math
import jax
import jax.numpy as jnp
import numpy as np
from jax import lax
from jax.sharding import PartitionSpec as P

HD = 128
QH = 32
KVH = 4
BLK = 128
STEPS = 4
SUF = 4096


def phase_table(half):
    index = np.arange(half)
    freq = 500000.0 ** (-2.0 * index / (2 * half))
    mult = np.floor(2.0**24 * freq / (2 * np.pi)).astype(np.int64)
    return ((mult >> 12).astype(np.int32), (mult & 4095).astype(np.int32))


def rotate(values, position):
    half = values.shape[-1] // 2
    high, low = phase_table(half)
    spot = position[..., None]
    first = spot * jnp.asarray(low, dtype=jnp.int32)
    second = spot * jnp.asarray(high, dtype=jnp.int32) % 4096
    turns = (first + second * 4096) % 16777216
    angle = turns.astype(values.dtype) * (2.0 * math.pi / 16777216.0)
    cosine = jnp.cos(angle)[..., None, :]
    sine = jnp.sin(angle)[..., None, :]
    lower = values[..., :half]
    upper = values[..., half:]
    return jnp.concatenate([lower * cosine - upper * sine, upper * cosine + lower * sine], -1)


def local(
    prefix_latent,
    block_order,
    key_up,
    value_up,
    queries,
    new_keys,
    new_values,
    suffix_keys,
    suffix_values,
    suffix_len,
):
    seq_count = lax.axis_size("seq")
    pre_rows = prefix_latent.shape[0]
    prefix = pre_rows * seq_count
    req_rows = queries.shape[0]
    group = QH // KVH
    scale = 1.0 / math.sqrt(HD)
    rows = jnp.arange(pre_rows, dtype=jnp.int32)
    key_pos = jnp.repeat(block_order, BLK) * BLK + rows % BLK
    keys = jnp.dot(prefix_latent, key_up, preferred_element_type=jnp.float32).reshape(
        pre_rows, KVH, HD
    )
    keys = rotate(keys, key_pos).astype(jnp.bfloat16)
    values = (
        jnp.dot(prefix_latent, value_up, preferred_element_type=jnp.float32)
        .astype(jnp.bfloat16)
        .reshape(pre_rows, KVH, HD)
    )
    step_index = jnp.arange(STEPS, dtype=jnp.int32)
    query_pos = prefix + suffix_len[:, None] + step_index[None, :]
    query_rot = rotate(
        queries.astype(jnp.float32).reshape(req_rows, STEPS, QH, HD), query_pos
    ).astype(jnp.bfloat16)
    new_rot = rotate(
        new_keys.astype(jnp.float32).reshape(req_rows, STEPS, KVH, HD), query_pos
    ).astype(jnp.bfloat16)

    def shard_part(query_block):
        count = query_block.shape[0]
        width = query_block.shape[1]
        split = query_block.reshape(count, width, KVH, group, HD)
        scores = (
            jnp.einsum("rtkgd,pkd->rtkgp", split, keys, preferred_element_type=jnp.float32) * scale
        )
        peak = jnp.max(scores, -1)
        expo = jnp.exp(scores - peak[..., None])
        total = jnp.sum(expo, -1)
        summed = jnp.einsum(
            "rtkgp,pkd->rtkgd",
            expo.astype(jnp.bfloat16),
            values,
            preferred_element_type=jnp.float32,
        )
        part = summed / total[..., None]
        return (
            part.reshape(count, width, QH * HD),
            peak.reshape(count, width, QH),
            total.reshape(count, width, QH),
        )

    def prefix_attention(selected):
        width = selected.shape[1]
        whole = lax.all_gather(selected, "seq", axis=0, tiled=True)
        count = whole.shape[0]
        per_block = math.gcd(count, max(1, 512 // (width * QH)))
        blocks = whole.reshape(count // per_block, per_block, width, QH * HD)
        parts, peaks, totals = lax.map(shard_part, blocks)
        parts = parts.reshape(count, width, QH * HD)
        peaks = peaks.reshape(count, width, QH)
        totals = totals.reshape(count, width, QH)
        got_parts, got_peaks, got_totals = (
            lax.all_to_all(parts[:, None], "seq", split_axis=0, concat_axis=1, tiled=True),
            lax.all_to_all(peaks[:, None], "seq", split_axis=0, concat_axis=1, tiled=True),
            lax.all_to_all(totals[:, None], "seq", split_axis=0, concat_axis=1, tiled=True),
        )
        highest = jnp.max(got_peaks, 1)
        factor = got_totals * jnp.exp(got_peaks - highest[:, None])
        numer = jnp.sum(
            factor[..., None] * got_parts.reshape(req_rows, seq_count, width, QH, HD), 1
        )
        denom = jnp.sum(factor, 1)
        return (highest, numer, denom)

    flat_queries = query_rot.reshape(req_rows, STEPS, QH * HD)
    results = [prefix_attention(flat_queries[:, which : which + 1]) for which in range(STEPS)]
    highest = jnp.concatenate([entry[0] for entry in results], 1)
    numer = jnp.concatenate([entry[1] for entry in results], 1)
    denom = jnp.concatenate([entry[2] for entry in results], 1)
    split = query_rot.reshape(req_rows, STEPS, KVH, group, HD)
    cache_keys = suffix_keys.reshape(req_rows, SUF, KVH, HD)
    cache_values = suffix_values.reshape(req_rows, SUF, KVH, HD)
    cache_scores = (
        jnp.einsum("rtkgd,rpkd->rtkgp", split, cache_keys, preferred_element_type=jnp.float32)
        * scale
    )
    live = jnp.arange(SUF, dtype=jnp.int32)[None, :] < suffix_len[:, None]
    cache_scores = jnp.where(live[:, None, None, None, :], cache_scores, -jnp.inf)
    fresh_keys = new_rot.reshape(req_rows, STEPS, KVH, HD)
    fresh_values = new_values.reshape(req_rows, STEPS, KVH, HD)
    fresh_scores = (
        jnp.einsum("rtkgd,rukd->rtkgu", split, fresh_keys, preferred_element_type=jnp.float32)
        * scale
    )
    causal = step_index[:, None] >= step_index[None, :]
    fresh_scores = jnp.where(causal[None, :, None, None, :], fresh_scores, -jnp.inf)
    local_peak = jnp.maximum(jnp.max(cache_scores, -1), jnp.max(fresh_scores, -1))
    cache_exp = jnp.exp(cache_scores - local_peak[..., None])
    fresh_exp = jnp.exp(fresh_scores - local_peak[..., None])
    local_total = jnp.sum(cache_exp, -1) + jnp.sum(fresh_exp, -1)
    local_numer = jnp.einsum(
        "rtkgp,rpkd->rtkgd",
        cache_exp.astype(jnp.bfloat16),
        cache_values,
        preferred_element_type=jnp.float32,
    )
    local_numer = local_numer + jnp.einsum(
        "rtkgu,rukd->rtkgd",
        fresh_exp.astype(jnp.bfloat16),
        fresh_values,
        preferred_element_type=jnp.float32,
    )
    local_peak = local_peak.reshape(req_rows, STEPS, QH)
    local_total = local_total.reshape(req_rows, STEPS, QH)
    local_numer = local_numer.reshape(req_rows, STEPS, QH, HD)
    biggest = jnp.maximum(highest, local_peak)
    prefix_weight = jnp.exp(highest - biggest)
    local_weight = jnp.exp(local_peak - biggest)
    result = (numer * prefix_weight[..., None] + local_numer * local_weight[..., None]) / (
        denom * prefix_weight + local_total * local_weight
    )[..., None]
    return result.reshape(req_rows, STEPS, QH * HD).astype(jnp.bfloat16)


def solution(mesh):
    placed = (
        P(("parts", "seq"), None),
        P(("parts", "seq")),
        P(),
        P(),
        P(("parts", "seq"), None, None),
        P(("parts", "seq"), None, None),
        P(("parts", "seq"), None, None),
        P(("parts", "seq"), None, None),
        P(("parts", "seq"), None, None),
        P(("parts", "seq")),
    )
    return jax.shard_map(
        local,
        mesh=mesh,
        in_specs=placed,
        out_specs=P(("parts", "seq"), None, None),
        check_vma=False,
    )
```

profile of v0, /device:TPU:0, one launch (start us, length us, event | category | flops | bytes accessed | tf_op | source)
XLA Modules:
  0.0 271.2 jit_solution(17228398530204130083)
XLA Ops:
  3.2 23.8 %all_gather.12 = bf16[16,1,4096]{2,1,0:T(2,128)(2,1)S(1)} all-gather(bf16[1,1,4096]{2,1,0:T(2,128)(2,1)S(1)} %get-tuple-element.75), channel_id=1, replica_groups=mesh['parts'=2,'seq'=16] {'seq'}, dimensions={0}, use_global_device_ids=true | all-gather | bytes 139264 | tf_op jit(solution)/shard_map/all_gather | solution.py:101
  32.5 3.7 %copy.155 = f32[1920,4,64]{2,0,1:T(8,128)} copy(f32[1920,4,64]{0,2,1:T(8,128)} %get-tuple-element.72) | data formatting | bytes 3932160
  36.1 3.7 %copy.156 = f32[1920,4,64]{2,0,1:T(8,128)} copy(f32[1920,4,64]{0,2,1:T(8,128)} %get-tuple-element.71) | data formatting | bytes 3932160
  39.9 4.3 %fusion.77 = (f32[1920,64]{1,0:T(8,128)S(1)}, f32[1920,64]{1,0:T(8,128)S(1)}) fusion(s32[64]{0:T(128)S(1)} %copy-done.20, s32[64]{0:T(128)S(1)} %copy-done.19, s32[1920]{0:T(1024)S(1)} %fusion.96), kind=kLoop, calls=%fused_computation.80 | loop fusion | flops 3440640 | bytes 991232 | tf_op jit(solution)/shard_map/cos | solution.py:31
  44.3 4.5 %subtract_convert_fusion = (bf16[1920,4,64]{2,0,1:T(8,128)(2,1)S(1)}, bf16[1920,4,64]{2,0,1:T(8,128)(2,1)S(1)}) fusion(f32[1920,4,64]{2,0,1:T(8,128)} %copy.156, f32[1920,4,64]{2,0,1:T(8,128)} %copy.155, f32[1920,64]{1,0:T(8,128)S(1)} %get-tuple-element.89, f32[1920,64]{1,0:T(8,128)S(1)} %get-tuple-element.88), kind=kLoop, calls=%fused_computation.20 | loop fusion | flops 3932160 | bytes 6881280 | tf_op jit(solution)/shard_map/convert.12
  54.4 3.7 %all-to-all-start = ((f32[16,1,1,32]{3,2,1,0:T(1,128)}), f32[16,1,1,32]{3,2,1,0:T(1,128)S(1)}, u32[]{:S(2)}, u32[]{:S(2)}) async-start(f32[16,1,1,32]{3,2,1,0:T(1,128)} %copy.101), calls=%async_computation | async-start | bytes 16384 | tf_op jit(solution)/shard_map/all_to_all | solution.py:112
  61.1 22.2 %all_gather.13 = bf16[16,1,4096]{2,1,0:T(2,128)(2,1)S(1)} all-gather(bf16[1,1,4096]{2,1,0:T(2,128)(2,1)S(1)} %get-tuple-element.85), channel_id=1, replica_groups=mesh['parts'=2,'seq'=16] {'seq'}, dimensions={0}, use_global_device_ids=true | all-gather | bytes 139264 | tf_op jit(solution)/shard_map/all_gather | solution.py:101
  87.2 18.2 %all_gather.14 = bf16[16,1,4096]{2,1,0:T(2,128)(2,1)S(1)} all-gather(bf16[1,1,4096]{2,1,0:T(2,128)(2,1)S(1)} %get-tuple-element.84), channel_id=1, replica_groups=mesh['parts'=2,'seq'=16] {'seq'}, dimensions={0}, use_global_device_ids=true | all-gather | bytes 139264 | tf_op jit(solution)/shard_map/all_gather | solution.py:101
  109.4 19.5 %all_gather.15 = bf16[16,1,4096]{2,1,0:T(2,128)(2,1)S(1)} all-gather(bf16[1,1,4096]{2,1,0:T(2,128)(2,1)S(1)} %get-tuple-element.76), channel_id=1, replica_groups=mesh['parts'=2,'seq'=16] {'seq'}, dimensions={0}, use_global_device_ids=true | all-gather | bytes 139264 | tf_op jit(solution)/shard_map/all_gather | solution.py:101
  133.5 6.9 %reshape.1695 = bf16[4096,4,128]{2,1,0:T(4,128)(2,1)} reshape(bf16[1,4096,512]{2,1,0:T(8,128)(2,1)} %param.23) | data formatting | bytes 8388608 | tf_op jit(solution)/shard_map/reshape.165
  140.4 3.8 %all-to-all-start.1 = ((f32[16,1,1,32]{3,2,1,0:T(1,128)}), f32[16,1,1,32]{3,2,1,0:T(1,128)S(1)}, u32[]{:S(2)}, u32[]{:S(2)}) async-start(f32[16,1,1,32]{3,2,1,0:T(1,128)} %copy.102), calls=%async_computation.1 | async-start | bytes 16384 | tf_op jit(solution)/shard_map/all_to_all | solution.py:111
  144.2 3.8 %fusion.125 = (f32[4,4,8]{2,0,1:T(4,128)S(1)}, f32[1,4,4,8,4096]{4,3,1,2,0:T(8,128)S(1)}) fusion(bf16[4096,4,128,1]{2,1,0,3:T(4,128)(2,1)} %bitcast.286, pred[4096]{0:T(1024)(128)(4,1)S(1)} %iota_compare_fusion, bf16[4,4,8,64]{3,2,1,0:T(8,128)(2,1)S(1)} %bitcast.301, bf16[4,4,8,64]{3,2,1,0:T(8,128)(2,1)S(1)} %bitcast.299), kind=kOutput, calls=%fused_computation.167 | convolution fusion | flops 135856000 | bytes 6328832 | tf_op jit(solution)/shard_map/rtkgd,rpkd->rtkgp/dot_general | solution.py:131
  150.6 4.1 %all-to-all-start.3 = ((f32[16,1,1,32]{3,2,1,0:T(1,128)}), f32[16,1,1,32]{3,2,1,0:T(1,128)S(1)}, u32[]{:S(2)}, u32[]{:S(2)}) async-start(f32[16,1,1,32]{3,2,1,0:T(1,128)} %copy.107), calls=%async_computation.3 | async-start | bytes 16384 | tf_op jit(solution)/shard_map/all_to_all | solution.py:112
  155.4 5.6 %all-to-all-done.3 = f32[16,1,1,32]{3,2,1,0:T(1,128)S(1)} async-done(((f32[16,1,1,32]{3,2,1,0:T(1,128)}), f32[16,1,1,32]{3,2,1,0:T(1,128)S(1)}, u32[]{:S(2)}, u32[]{:S(2)}) %all-to-all-start.3) | async-done | bytes 2080 | tf_op jit(solution)/shard_map/all_to_all | solution.py:112
  161.0 3.5 %all-to-all-start.4 = ((f32[16,1,1,32]{3,2,1,0:T(1,128)}), f32[16,1,1,32]{3,2,1,0:T(1,128)S(1)}, u32[]{:S(2)}, u32[]{:S(2)}) async-start(f32[16,1,1,32]{3,2,1,0:T(1,128)} %copy.108), calls=%async_computation.4 | async-start | bytes 16384 | tf_op jit(solution)/shard_map/all_to_all | solution.py:111
  165.3 5.6 %all-to-all-done.4 = f32[16,1,1,32]{3,2,1,0:T(1,128)S(1)} async-done(((f32[16,1,1,32]{3,2,1,0:T(1,128)}), f32[16,1,1,32]{3,2,1,0:T(1,128)S(1)}, u32[]{:S(2)}, u32[]{:S(2)}) %all-to-all-start.4) | async-done | bytes 2080 | tf_op jit(solution)/shard_map/all_to_all | solution.py:111
  170.9 3.5 %all-to-all-start.6 = ((f32[16,1,1,32]{3,2,1,0:T(1,128)}), f32[16,1,1,32]{3,2,1,0:T(1,128)S(1)}, u32[]{:S(2)}, u32[]{:S(2)}) async-start(f32[16,1,1,32]{3,2,1,0:T(1,128)} %copy.113), calls=%async_computation.6 | async-start | bytes 16384 | tf_op jit(solution)/shard_map/all_to_all | solution.py:112
  175.1 5.6 %all-to-all-done.6 = f32[16,1,1,32]{3,2,1,0:T(1,128)S(1)} async-done(((f32[16,1,1,32]{3,2,1,0:T(1,128)}), f32[16,1,1,32]{3,2,1,0:T(1,128)S(1)}, u32[]{:S(2)}, u32[]{:S(2)}) %all-to-all-start.6) | async-done | bytes 2080 | tf_op jit(solution)/shard_map/all_to_all | solution.py:112
  181.3 3.5 %all-to-all-start.7 = ((f32[16,1,1,32]{3,2,1,0:T(1,128)}), f32[16,1,1,32]{3,2,1,0:T(1,128)S(1)}, u32[]{:S(2)}, u32[]{:S(2)}) async-start(f32[16,1,1,32]{3,2,1,0:T(1,128)} %copy.114), calls=%async_computation.7 | async-start | bytes 16384 | tf_op jit(solution)/shard_map/all_to_all | solution.py:111
  185.8 6.9 %reshape.1699 = bf16[4096,4,128]{2,1,0:T(4,128)(2,1)} reshape(bf16[1,4096,512]{2,1,0:T(8,128)(2,1)} %param.24) | data formatting | bytes 8388608 | tf_op jit(solution)/shard_map/reshape.180
  192.7 6.0 %all-to-all-start.9 = ((f32[16,1,1,32]{3,2,1,0:T(1,128)}), f32[16,1,1,32]{3,2,1,0:T(1,128)S(1)}, u32[]{:S(2)}, u32[]{:S(2)}) async-start(f32[16,1,1,32]{3,2,1,0:T(1,128)} %copy.119), calls=%async_computation.9 | async-start | bytes 16384 | tf_op jit(solution)/shard_map/all_to_all | solution.py:112
  198.7 3.0 %fusion.3 = f32[4,4,8,128]{3,2,1,0:T(8,128)S(1)} fusion(bf16[4096,4,128,1]{2,1,0,3:T(4,128)(2,1)} %bitcast.285, f32[1,4,4,8,4096]{4,3,1,2,0:T(8,128)S(1)} %get-tuple-element.117, f32[4,4,8]{2,0,1:T(4,128)S(1)} %max.48), kind=kOutput, calls=%fused_computation.4 | convolution fusion | flops 135266304 | bytes 6357504 | tf_op jit(solution)/shard_map/rtkgp,rpkd->rtkgd/dot_general | solution.py:148
  205.7 3.5 %all-to-all-start.10 = ((f32[16,1,1,32]{3,2,1,0:T(1,128)}), f32[16,1,1,32]{3,2,1,0:T(1,128)S(1)}, u32[]{:S(2)}, u32[]{:S(2)}) async-start(f32[16,1,1,32]{3,2,1,0:T(1,128)} %copy.120), calls=%async_computation.10 | async-start | bytes 16384 | tf_op jit(solution)/shard_map/all_to_all | solution.py:111
  210.4 5.1 %all-to-all-done.10 = f32[16,1,1,32]{3,2,1,0:T(1,128)S(1)} async-done(((f32[16,1,1,32]{3,2,1,0:T(1,128)}), f32[16,1,1,32]{3,2,1,0:T(1,128)S(1)}, u32[]{:S(2)}, u32[]{:S(2)}) %all-to-all-start.10) | async-done | bytes 2080 | tf_op jit(solution)/shard_map/all_to_all | solution.py:111
  215.5 3.5 %all-to-all-start.2 = ((f32[16,1,1,4096]{3,1,2,0:T(1,128)}), f32[16,1,1,4096]{3,1,2,0:T(1,128)S(1)}, u32[]{:S(2)}, u32[]{:S(2)}) async-start(f32[16,1,1,4096]{3,1,2,0:T(1,128)} %bitcast.19), calls=%async_computation.2 | async-start | bytes 524288 | tf_op jit(solution)/shard_map/all_to_all | solution.py:110
  222.1 7.0 %all-to-all-done.2 = f32[16,1,1,4096]{3,1,2,0:T(1,128)S(1)} async-done(((f32[16,1,1,4096]{3,1,2,0:T(1,128)}), f32[16,1,1,4096]{3,1,2,0:T(1,128)S(1)}, u32[]{:S(2)}, u32[]{:S(2)}) %all-to-all-start.2) | async-done | bytes 262176 | tf_op jit(solution)/shard_map/all_to_all | solution.py:110
  229.1 3.5 %all-to-all-start.5 = ((f32[16,1,1,4096]{3,1,2,0:T(1,128)}), f32[16,1,1,4096]{3,1,2,0:T(1,128)S(1)}, u32[]{:S(2)}, u32[]{:S(2)}) async-start(f32[16,1,1,4096]{3,1,2,0:T(1,128)} %bitcast.35), calls=%async_computation.5 | async-start | bytes 524288 | tf_op jit(solution)/shard_map/all_to_all | solution.py:110
  233.4 9.3 %all-to-all-done.5 = f32[16,1,1,4096]{3,1,2,0:T(1,128)S(1)} async-done(((f32[16,1,1,4096]{3,1,2,0:T(1,128)}), f32[16,1,1,4096]{3,1,2,0:T(1,128)S(1)}, u32[]{:S(2)}, u32[]{:S(2)}) %all-to-all-start.5) | async-done | bytes 262176 | tf_op jit(solution)/shard_map/all_to_all | solution.py:110
  242.6 3.5 %all-to-all-start.8 = ((f32[16,1,1,4096]{3,1,2,0:T(1,128)}), f32[16,1,1,4096]{3,1,2,0:T(1,128)S(1)}, u32[]{:S(2)}, u32[]{:S(2)}) async-start(f32[16,1,1,4096]{3,1,2,0:T(1,128)} %bitcast.50), calls=%async_computation.8 | async-start | bytes 524288 | tf_op jit(solution)/shard_map/all_to_all | solution.py:110
  247.6 8.6 %all-to-all-done.8 = f32[16,1,1,4096]{3,1,2,0:T(1,128)S(1)} async-done(((f32[16,1,1,4096]{3,1,2,0:T(1,128)}), f32[16,1,1,4096]{3,1,2,0:T(1,128)S(1)}, u32[]{:S(2)}, u32[]{:S(2)}) %all-to-all-start.8) | async-done | bytes 262176 | tf_op jit(solution)/shard_map/all_to_all | solution.py:110
  256.2 3.5 %all-to-all-start.11 = ((f32[16,1,1,4096]{3,1,2,0:T(1,128)}), f32[16,1,1,4096]{3,1,2,0:T(1,128)S(1)}, u32[]{:S(2)}, u32[]{:S(2)}) async-start(f32[16,1,1,4096]{3,1,2,0:T(1,128)} %bitcast.65), calls=%async_computation.11 | async-start | bytes 524288 | tf_op jit(solution)/shard_map/all_to_all | solution.py:110
  261.0 8.7 %all-to-all-done.11 = f32[16,1,1,4096]{3,1,2,0:T(1,128)S(1)} async-done(((f32[16,1,1,4096]{3,1,2,0:T(1,128)}), f32[16,1,1,4096]{3,1,2,0:T(1,128)S(1)}, u32[]{:S(2)}, u32[]{:S(2)}) %all-to-all-start.11) | async-done | bytes 262176 | tf_op jit(solution)/shard_map/all_to_all | solution.py:110
  (145 shorter events, 48.3 us)
Async XLA Ops:
  0.0 27.7 %copy-start = (bf16[1920,512]{1,0:T(8,128)(2,1)S(1)}, bf16[1920,512]{1,0:T(8,128)(2,1)}, u32[]{:S(2)}) copy-start(bf16[1920,512]{1,0:T(8,128)(2,1)} %param.16) | copy-start | bytes 5898244
  36.1 3.7 %copy-start.22 = (s32[15]{0:T(128)S(1)}, s32[15]{0:T(128)}, u32[]{:S(2)}) copy-start(s32[15]{0:T(128)} %param.17) | copy-start | bytes 184
  36.1 3.8 %copy-start.19 = (s32[64]{0:T(128)S(1)}, s32[64]{0:T(128)}, u32[]{:S(2)}) copy-start(s32[64]{0:T(128)} %constant.146.clone) | copy-start | bytes 772
  36.1 3.8 %copy-start.20 = (s32[64]{0:T(128)S(1)}, s32[64]{0:T(128)}, u32[]{:S(2)}) copy-start(s32[64]{0:T(128)} %constant.147.clone) | copy-start | bytes 772
  51.1 1.9 copy-start.4
  51.1 7.0 %copy-start.21 = (bf16[512,512]{1,0:T(8,128)(2,1)S(1)}, bf16[512,512]{1,0:T(8,128)(2,1)}, u32[]{:S(2)}) copy-start(bf16[512,512]{1,0:T(8,128)(2,1)} %param.19) | copy-start | bytes 1572868
  54.4 86.0 %all-to-all-start = ((f32[16,1,1,32]{3,2,1,0:T(1,128)}), f32[16,1,1,32]{3,2,1,0:T(1,128)S(1)}, u32[]{:S(2)}, u32[]{:S(2)}) async-start(f32[16,1,1,32]{3,2,1,0:T(1,128)} %copy.101), calls=%async_computation | async-start | bytes 16384 | tf_op jit(solution)/shard_map/all_to_all | solution.py:112
  58.1 2.1 copy-start.5
  59.4 1.7 copy-start.23
  59.4 24.6 %copy-start.3 = (bf16[1920,4,128,1]{2,0,3,1:T(8,128)(2,1)S(1)}, bf16[1920,4,128,1]{2,0,3,1:T(8,128)(2,1)}, u32[]{:S(2)}) copy-start(bf16[1920,4,128,1]{2,0,3,1:T(8,128)(2,1)} %copy-done.2) | copy-start | bytes 5898244
  84.8 1.5 copy-start.24
  86.4 20.6 %copy-start.11 = (f32[16,4,8]{0,2,1:T(8,128)}, f32[16,4,8]{0,2,1:T(8,128)S(1)}, u32[]{:S(2)}) copy-start(f32[16,4,8]{0,2,1:T(8,128)S(1)} %fusion.13) | copy-start | bytes 6148
  140.4 7.6 %copy-start.12 = (f32[16,4,8]{0,2,1:T(8,128)S(1)}, f32[16,4,8]{0,2,1:T(8,128)}, u32[]{:S(2)}) copy-start(f32[16,4,8]{0,2,1:T(8,128)} %copy-done.11) | copy-start | bytes 6148
  140.4 14.3 %copy-start.17 = (bf16[1,4,512]{2,1,0:T(4,128)(2,1)S(1)}, bf16[1,4,512]{2,1,0:T(4,128)(2,1)}, u32[]{:S(2)}) copy-start(bf16[1,4,512]{2,1,0:T(4,128)(2,1)} %param.21) | copy-start | bytes 12292
  140.4 24.1 %copy-start.14 = (f32[4,64]{1,0:T(4,128)S(1)}, f32[4,64]{1,0:T(4,128)}, u32[]{:S(2)}) copy-start(f32[4,64]{1,0:T(4,128)} %copy-done.13) | copy-start | bytes 3076
  140.4 24.1 %copy-start.16 = (f32[4,64]{1,0:T(4,128)S(1)}, f32[4,64]{1,0:T(4,128)}, u32[]{:S(2)}) copy-start(f32[4,64]{1,0:T(4,128)} %copy-done.15) | copy-start | bytes 3076
  140.4 10.2 %all-to-all-start.1 = ((f32[16,1,1,32]{3,2,1,0:T(1,128)}), f32[16,1,1,32]{3,2,1,0:T(1,128)S(1)}, u32[]{:S(2)}, u32[]{:S(2)}) async-start(f32[16,1,1,32]{3,2,1,0:T(1,128)} %copy.102), calls=%async_computation.1 | async-start | bytes 16384 | tf_op jit(solution)/shard_map/all_to_all | solution.py:111
  150.6 10.4 %all-to-all-start.3 = ((f32[16,1,1,32]{3,2,1,0:T(1,128)}), f32[16,1,1,32]{3,2,1,0:T(1,128)S(1)}, u32[]{:S(2)}, u32[]{:S(2)}) async-start(f32[16,1,1,32]{3,2,1,0:T(1,128)} %copy.107), calls=%async_computation.3 | async-start | bytes 16384 | tf_op jit(solution)/shard_map/all_to_all | solution.py:112
  161.0 23.7 %copy-start.6 = (f32[16,1,1,32]{3,2,1,0:T(1,128)}, f32[16,1,1,32]{3,2,1,0:T(1,128)S(1)}, u32[]{:S(2)}) copy-start(f32[16,1,1,32]{3,2,1,0:T(1,128)S(1)} %all-to-all-done.3) | copy-start | bytes 6148
  161.0 9.9 %all-to-all-start.4 = ((f32[16,1,1,32]{3,2,1,0:T(1,128)}), f32[16,1,1,32]{3,2,1,0:T(1,128)S(1)}, u32[]{:S(2)}, u32[]{:S(2)}) async-start(f32[16,1,1,32]{3,2,1,0:T(1,128)} %copy.108), calls=%async_computation.4 | async-start | bytes 16384 | tf_op jit(solution)/shard_map/all_to_all | solution.py:111
  170.9 9.8 %all-to-all-start.6 = ((f32[16,1,1,32]{3,2,1,0:T(1,128)}), f32[16,1,1,32]{3,2,1,0:T(1,128)S(1)}, u32[]{:S(2)}, u32[]{:S(2)}) async-start(f32[16,1,1,32]{3,2,1,0:T(1,128)} %copy.113), calls=%async_computation.6 | async-start | bytes 16384 | tf_op jit(solution)/shard_map/all_to_all | solution.py:112
  181.3 11.5 %all-to-all-start.7 = ((f32[16,1,1,32]{3,2,1,0:T(1,128)}), f32[16,1,1,32]{3,2,1,0:T(1,128)S(1)}, u32[]{:S(2)}, u32[]{:S(2)}) async-start(f32[16,1,1,32]{3,2,1,0:T(1,128)} %copy.114), calls=%async_computation.7 | async-start | bytes 16384 | tf_op jit(solution)/shard_map/all_to_all | solution.py:111
  192.7 12.3 %all-to-all-start.9 = ((f32[16,1,1,32]{3,2,1,0:T(1,128)}), f32[16,1,1,32]{3,2,1,0:T(1,128)S(1)}, u32[]{:S(2)}, u32[]{:S(2)}) async-start(f32[16,1,1,32]{3,2,1,0:T(1,128)} %copy.119), calls=%async_computation.9 | async-start | bytes 16384 | tf_op jit(solution)/shard_map/all_to_all | solution.py:112
  201.8 19.9 %copy-start.18 = (bf16[1,4,512]{2,1,0:T(4,128)(2,1)S(1)}, bf16[1,4,512]{2,1,0:T(4,128)(2,1)}, u32[]{:S(2)}) copy-start(bf16[1,4,512]{2,1,0:T(4,128)(2,1)} %param.22) | copy-start | bytes 12292
  201.8 20.3 %copy-start.7 = (f32[16,1,1,32]{3,2,1,0:T(1,128)S(1)}, f32[16,1,1,32]{3,2,1,0:T(1,128)}, u32[]{:S(2)}) copy-start(f32[16,1,1,32]{3,2,1,0:T(1,128)} %copy-done.6) | copy-start | bytes 6148
  201.8 20.3 %copy-start.9 = (f32[16,1,1,32]{3,2,1,0:T(1,128)S(1)}, f32[16,1,1,32]{3,2,1,0:T(1,128)}, u32[]{:S(2)}) copy-start(f32[16,1,1,32]{3,2,1,0:T(1,128)} %copy-done.8) | copy-start | bytes 6148
  205.7 9.9 %all-to-all-start.10 = ((f32[16,1,1,32]{3,2,1,0:T(1,128)}), f32[16,1,1,32]{3,2,1,0:T(1,128)S(1)}, u32[]{:S(2)}, u32[]{:S(2)}) async-start(f32[16,1,1,32]{3,2,1,0:T(1,128)} %copy.120), calls=%async_computation.10 | async-start | bytes 16384 | tf_op jit(solution)/shard_map/all_to_all | solution.py:111
  215.5 13.5 %all-to-all-start.2 = ((f32[16,1,1,4096]{3,1,2,0:T(1,128)}), f32[16,1,1,4096]{3,1,2,0:T(1,128)S(1)}, u32[]{:S(2)}, u32[]{:S(2)}) async-start(f32[16,1,1,4096]{3,1,2,0:T(1,128)} %bitcast.19), calls=%async_computation.2 | async-start | bytes 524288 | tf_op jit(solution)/shard_map/all_to_all | solution.py:110
  219.1 52.2 %copy-start.1 = (bf16[1920,512]{1,0:T(8,128)(2,1)S(1)}, bf16[1920,512]{1,0:T(8,128)(2,1)}, u32[]{:S(2)}) copy-start(bf16[1920,512]{1,0:T(8,128)(2,1)} %param.16) | copy-start | bytes 5898244
  229.1 13.5 %all-to-all-start.5 = ((f32[16,1,1,4096]{3,1,2,0:T(1,128)}), f32[16,1,1,4096]{3,1,2,0:T(1,128)S(1)}, u32[]{:S(2)}, u32[]{:S(2)}) async-start(f32[16,1,1,4096]{3,1,2,0:T(1,128)} %bitcast.35), calls=%async_computation.5 | async-start | bytes 524288 | tf_op jit(solution)/shard_map/all_to_all | solution.py:110
  242.6 13.5 %all-to-all-start.8 = ((f32[16,1,1,4096]{3,1,2,0:T(1,128)}), f32[16,1,1,4096]{3,1,2,0:T(1,128)S(1)}, u32[]{:S(2)}, u32[]{:S(2)}) async-start(f32[16,1,1,4096]{3,1,2,0:T(1,128)} %bitcast.50), calls=%async_computation.8 | async-start | bytes 524288 | tf_op jit(solution)/shard_map/all_to_all | solution.py:110
  256.2 13.5 %all-to-all-start.11 = ((f32[16,1,1,4096]{3,1,2,0:T(1,128)}), f32[16,1,1,4096]{3,1,2,0:T(1,128)S(1)}, u32[]{:S(2)}, u32[]{:S(2)}) async-start(f32[16,1,1,4096]{3,1,2,0:T(1,128)} %bitcast.65), calls=%async_computation.11 | async-start | bytes 524288 | tf_op jit(solution)/shard_map/all_to_all | solution.py:110
  (7 other events, 6.7 us)
where the time goes:
time: 273 us; the launch traced here: 271 us
  blocking collectives  83.6 us (31%)
  waiting for transfers between devices  59.9 us (22%)
  starting transfers between devices  45.6 us (17%)
  local copies, waits for them, and re-layouts  40.9 us (15%)
  other arithmetic  22.1 us (8%)
  matrix products  17.6 us (6%)
    all_gather x4, blocking collectives, prefix_attention(): whole = lax.all_gather(selected, 'seq', axis=0, tiled=True)  83.6 us
    all_to_all x4, waiting for transfers between devices, prefix_attention(): lax.all_to_all(parts[:, None], 'seq', split_axis=0, concat_axis=1, tiled=...  33.5 us
    all_to_all x4, starting transfers between devices, prefix_attention(): lax.all_to_all(totals[:, None], 'seq', split_axis=0, concat_axis=1, tiled...  17.2 us
    unnamed x61, local copies, waits for them, and re-layouts  14.6 us
    all_to_all x4, starting transfers between devices, prefix_attention(): lax.all_to_all(peaks[:, None], 'seq', split_axis=0, concat_axis=1, tiled=...  14.3 us
    all_to_all x4, starting transfers between devices, prefix_attention(): lax.all_to_all(parts[:, None], 'seq', split_axis=0, concat_axis=1, tiled=...  14.1 us
    another operation x2, local copies, waits for them, and re-layouts  13.9 us
    all_to_all x4, waiting for transfers between devices, prefix_attention(): lax.all_to_all(totals[:, None], 'seq', split_axis=0, concat_axis=1, tiled...  13.8 us
  transfers between devices with their start and end apart: 12, of which 10 were waited for; matrix products, arithmetic and copies ran while one was open for 17% of the time, Pallas kernels for 0%

commit v1 on v0

--- a/solution.py
+++ b/solution.py
@@ -98,7 +98,13 @@
 
     def prefix_attention(selected):
         width = selected.shape[1]
-        whole = lax.all_gather(selected, "seq", axis=0, tiled=True)
+        n_dev = lax.axis_size("seq")
+        block, pieces = (selected, [selected])
+        for _ in range(n_dev - 1):
+            block = lax.ppermute(block, "seq", [(i, (i + 1) % n_dev) for i in range(n_dev)])
+            pieces.insert(0, block)
+        row_of_blocks = jnp.concatenate(pieces, axis=0)
+        whole = jnp.roll(row_of_blocks, (lax.axis_index("seq") + 1) * selected.shape[0], axis=0)
         count = whole.shape[0]
         per_block = math.gcd(count, max(1, 512 // (width * QH)))
         blocks = whole.reshape(count // per_block, per_block, width, QH * HD)

time: 273 us -> 260 us (0.952)
  blocking collectives: 83.6 us -> 0 us
  waiting for transfers between devices: 59.9 us -> 91.1 us
  starting transfers between devices: 45.6 us -> 71.7 us
  matrix products: 17.6 us -> 31.6 us
  local copies, waits for them, and re-layouts: 40.9 us -> 37.9 us
  other arithmetic: 22.1 us -> 24.9 us
    all_gather x4 -> x0, blocking collectives: 83.6 us -> none  [prefix_attention(): whole = lax.all_gather(selected, 'seq', axis=0, tiled=True)]
    ppermute x0 -> x60, waiting for transfers between devices: none -> 35.3 us  [prefix_attention(): lax.ppermute(block, 'seq', [(i, (i + 1) % n_dev) for i in range(n_dev)])]
    ppermute x0 -> x60, starting transfers between devices: none -> 27.3 us  [prefix_attention(): lax.ppermute(block, 'seq', [(i, (i + 1) % n_dev) for i in range(n_dev)])]
    dot_general x4, matrix products: 3.38 us -> 10.4 us  [shard_part(): jnp.einsum('rtkgp,pkd->rtkgd', expo.astype(jnp.bfloat16), values, preferr...]
    unnamed x61 -> x35, local copies, waits for them, and re-layouts: 14.6 us -> 10.1 us
    reduce_sum x4, other arithmetic: 3.1 us -> 7.33 us  [shard_part(): total = jnp.sum(expo, -1)]
    all_to_all x4, waiting for transfers between devices: 13.8 us -> 9.87 us  [prefix_attention(): lax.all_to_all(totals[:, None], 'seq', split_axis=0, concat_axis=1, tiled...]
    dot_general x4, matrix products: 3.18 us -> 6.76 us  [shard_part(): jnp.einsum('rtkgd,pkd->rtkgp', split, keys, preferred_element_type=jnp.fl...]
  transfers between devices with their start and end apart: 12 -> 72, of which waited for: 10 -> 42; matrix products, arithmetic and copies ran while one was open for 17% -> 34% of each run, Pallas kernels for 0% -> 0%
where the time goes in v1:
time: 260 us; the launch traced here: 259 us
  waiting for transfers between devices  91.1 us (35%)
  starting transfers between devices  71.7 us (28%)
  local copies, waits for them, and re-layouts  37.9 us (15%)
  matrix products  31.6 us (12%)
  other arithmetic  24.9 us (10%)
    ppermute x60, waiting for transfers between devices, prefix_attention(): lax.ppermute(block, 'seq', [(i, (i + 1) % n_dev) for i in range(n_dev)])  35.3 us
    all_to_all x4, waiting for transfers between devices, prefix_attention(): lax.all_to_all(parts[:, None], 'seq', split_axis=0, concat_axis=1, tiled=...  32.3 us
    ppermute x60, starting transfers between devices, prefix_attention(): lax.ppermute(block, 'seq', [(i, (i + 1) % n_dev) for i in range(n_dev)])  27.3 us
    all_to_all x4, starting transfers between devices, prefix_attention(): lax.all_to_all(totals[:, None], 'seq', split_axis=0, concat_axis=1, tiled...  15.3 us
    all_to_all x4, starting transfers between devices, prefix_attention(): lax.all_to_all(peaks[:, None], 'seq', split_axis=0, concat_axis=1, tiled=...  15.1 us
    all_to_all x4, starting transfers between devices, prefix_attention(): lax.all_to_all(parts[:, None], 'seq', split_axis=0, concat_axis=1, tiled=...  14.1 us
    another operation x2, local copies, waits for them, and re-layouts  13.8 us
    all_to_all x4, waiting for transfers between devices, prefix_attention(): lax.all_to_all(peaks[:, None], 'seq', split_axis=0, concat_axis=1, tiled=...  13.7 us
  transfers between devices with their start and end apart: 72, of which 42 were waited for; matrix products, arithmetic and copies ran while one was open for 34% of the time, Pallas kernels for 0%

profile of v1, /device:TPU:0, one launch (start us, length us, event | category | flops | bytes accessed | tf_op | source)
XLA Modules:
  0.0 258.7 jit_solution(16457712735561909151)
XLA Ops:
  13.9 5.6 %fusion.77 = (f32[1920,64]{1,0:T(8,128)S(1)}, f32[1920,64]{1,0:T(8,128)}) fusion(s32[64]{0:T(128)S(1)} %copy-done.9, s32[64]{0:T(128)S(1)} %copy-done.8, s32[1920]{0:T(1024)S(1)} %fusion.104), kind=kLoop, calls=%fused_computation.80 | loop fusion | flops 3440640 | bytes 991232 | tf_op jit(solution)/shard_map/cos | solution.py:31
  19.5 3.6 %copy.163 = f32[1920,4,64]{2,0,1:T(8,128)} copy(f32[1920,4,64]{0,2,1:T(8,128)} %get-tuple-element.73) | data formatting | bytes 3932160
  23.2 3.7 %copy.164 = f32[1920,4,64]{2,0,1:T(8,128)} copy(f32[1920,4,64]{0,2,1:T(8,128)} %get-tuple-element.72) | data formatting | bytes 3932160
  30.1 6.4 %subtract_convert_fusion = (bf16[1920,4,64]{2,0,1:T(8,128)(2,1)}, bf16[1920,4,64]{2,0,1:T(8,128)(2,1)}) fusion(f32[1920,4,64]{2,0,1:T(8,128)} %copy.164, f32[1920,4,64]{2,0,1:T(8,128)} %copy.163, f32[1920,64]{1,0:T(8,128)} %get-tuple-element.90, f32[1920,64]{1,0:T(8,128)S(1)} %get-tuple-element.89), kind=kLoop, calls=%fused_computation.20 | loop fusion | flops 3932160 | bytes 6881280 | tf_op jit(solution)/shard_map/convert.12
  39.8 6.9 %reshape.1695 = bf16[4096,4,128]{2,1,0:T(4,128)(2,1)} reshape(bf16[1,4096,512]{2,1,0:T(8,128)(2,1)} %param.25) | data formatting | bytes 8388608 | tf_op jit(solution)/shard_map/reshape.165
  48.7 5.1 %fusion.133 = (f32[4,4,8]{2,0,1:T(4,128)S(1)}, f32[1,4,4,8,4096]{4,3,1,2,0:T(8,128)}) fusion(bf16[4096,4,128,1]{2,1,0,3:T(4,128)(2,1)} %bitcast.298, pred[4096]{0:T(1024)(128)(4,1)S(1)} %iota_compare_fusion, bf16[4,4,8,64]{3,2,1,0:T(8,128)(2,1)S(1)} %bitcast.309, bf16[4,4,8,64]{3,2,1,0:T(8,128)(2,1)S(1)} %bitcast.307), kind=kOutput, calls=%fused_computation.183 | convolution fusion | flops 135856000 | bytes 6328832 | tf_op jit(solution)/shard_map/rtkgd,rpkd->rtkgp/dot_general | solution.py:137
  61.5 4.0 %collective-permute-done.35 = bf16[1,1,4096]{2,0,1:T(2,128)(2,1)S(1)} collective-permute-done((bf16[1,1,4096]{2,0,1:T(2,128)(2,1)S(1)}, bf16[1,1,4096]{2,0,1:T(2,128)(2,1)S(1)}, u32[]{:S(2)}, u32[]{:S(2)}) %collective-permute-start.35) | collective-permute-done | bytes 8224 | tf_op jit(solution)/shard_map/ppermute | solution.py:104
  67.3 4.0 %collective-permute-done.36 = bf16[1,1,4096]{2,0,1:T(2,128)(2,1)S(1)} collective-permute-done((bf16[1,1,4096]{2,0,1:T(2,128)(2,1)S(1)}, bf16[1,1,4096]{2,0,1:T(2,128)(2,1)S(1)}, u32[]{:S(2)}, u32[]{:S(2)}) %collective-permute-start.36) | collective-permute-done | bytes 8224 | tf_op jit(solution)/shard_map/ppermute | solution.py:104
  73.5 6.9 %reshape.1699 = bf16[4096,4,128]{2,1,0:T(4,128)(2,1)} reshape(bf16[1,4096,512]{2,1,0:T(8,128)(2,1)} %param.26) | data formatting | bytes 8388608 | tf_op jit(solution)/shard_map/reshape.180
  80.7 3.7 %fusion.3 = f32[4,4,8,128]{3,2,1,0:T(8,128)S(1)} fusion(bf16[4096,4,128,1]{2,1,0,3:T(4,128)(2,1)} %bitcast.297, f32[1,4,4,8,4096]{4,3,1,2,0:T(8,128)} %get-tuple-element.118, f32[4,4,8]{2,0,1:T(4,128)S(1)} %max.48), kind=kOutput, calls=%fused_computation.4 | convolution fusion | flops 135266304 | bytes 6357504 | tf_op jit(solution)/shard_map/rtkgp,rpkd->rtkgd/dot_general | solution.py:154
  93.0 3.9 %collective-permute-start.26 = (bf16[1,1,4096]{2,0,1:T(2,128)(2,1)S(1)}, bf16[1,1,4096]{2,0,1:T(2,128)(2,1)S(1)}, u32[]{:S(2)}, u32[]{:S(2)}) collective-permute-start(bf16[1,1,4096]{2,0,1:T(2,128)(2,1)S(1)} %collective-permute-done.25), channel_id=1, source_target_pairs={{0,1},{1,2},{2,3},{3,4},{4,5},{5,6},{6,7},{7,8},{8,9},{9,10},{10,1... | collective-permute-start | bytes 24584 | tf_op jit(solution)/shard_map/ppermute | solution.py:104
  106.0 3.8 %collective-permute-done.42 = bf16[1,1,4096]{2,0,1:T(2,128)(2,1)S(1)} collective-permute-done((bf16[1,1,4096]{2,0,1:T(2,128)(2,1)S(1)}, bf16[1,1,4096]{2,0,1:T(2,128)(2,1)S(1)}, u32[]{:S(2)}, u32[]{:S(2)}) %collective-permute-start.42) | collective-permute-done | bytes 8224 | tf_op jit(solution)/shard_map/ppermute | solution.py:104
  111.9 3.7 %collective-permute-done.43 = bf16[1,1,4096]{2,0,1:T(2,128)(2,1)S(1)} collective-permute-done((bf16[1,1,4096]{2,0,1:T(2,128)(2,1)S(1)}, bf16[1,1,4096]{2,0,1:T(2,128)(2,1)S(1)}, u32[]{:S(2)}, u32[]{:S(2)}) %collective-permute-start.43) | collective-permute-done | bytes 8224 | tf_op jit(solution)/shard_map/ppermute | solution.py:104
  122.2 4.6 %all-to-all-start = ((f32[16,1,1,32]{3,2,1,0:T(1,128)}), f32[16,1,1,32]{3,2,1,0:T(1,128)S(1)}, u32[]{:S(2)}, u32[]{:S(2)}) async-start(f32[16,1,1,32]{3,2,1,0:T(1,128)} %copy.106), calls=%async_computation | async-start | bytes 16384 | tf_op jit(solution)/shard_map/all_to_all | solution.py:118
  133.1 4.7 %all-to-all-start.1 = ((f32[16,1,1,32]{3,2,1,0:T(1,128)}), f32[16,1,1,32]{3,2,1,0:T(1,128)S(1)}, u32[]{:S(2)}, u32[]{:S(2)}) async-start(f32[16,1,1,32]{3,2,1,0:T(1,128)} %copy.107), calls=%async_computation.1 | async-start | bytes 16384 | tf_op jit(solution)/shard_map/all_to_all | solution.py:117
  138.7 5.5 %all-to-all-done.1 = f32[16,1,1,32]{3,2,1,0:T(1,128)S(1)} async-done(((f32[16,1,1,32]{3,2,1,0:T(1,128)}), f32[16,1,1,32]{3,2,1,0:T(1,128)S(1)}, u32[]{:S(2)}, u32[]{:S(2)}) %all-to-all-start.1) | async-done | bytes 2080 | tf_op jit(solution)/shard_map/all_to_all | solution.py:117
  144.2 3.7 %all-to-all-start.3 = ((f32[16,1,1,32]{3,2,1,0:T(1,128)}), f32[16,1,1,32]{3,2,1,0:T(1,128)S(1)}, u32[]{:S(2)}, u32[]{:S(2)}) async-start(f32[16,1,1,32]{3,2,1,0:T(1,128)} %copy.113), calls=%async_computation.3 | async-start | bytes 16384 | tf_op jit(solution)/shard_map/all_to_all | solution.py:118
  154.0 3.4 %all-to-all-start.4 = ((f32[16,1,1,32]{3,2,1,0:T(1,128)}), f32[16,1,1,32]{3,2,1,0:T(1,128)S(1)}, u32[]{:S(2)}, u32[]{:S(2)}) async-start(f32[16,1,1,32]{3,2,1,0:T(1,128)} %copy.114), calls=%async_computation.4 | async-start | bytes 16384 | tf_op jit(solution)/shard_map/all_to_all | solution.py:117
  163.8 3.5 %all-to-all-start.6 = ((f32[16,1,1,32]{3,2,1,0:T(1,128)}), f32[16,1,1,32]{3,2,1,0:T(1,128)S(1)}, u32[]{:S(2)}, u32[]{:S(2)}) async-start(f32[16,1,1,32]{3,2,1,0:T(1,128)} %copy.120), calls=%async_computation.6 | async-start | bytes 16384 | tf_op jit(solution)/shard_map/all_to_all | solution.py:118
  170.5 3.0 %all-to-all-done.6 = f32[16,1,1,32]{3,2,1,0:T(1,128)S(1)} async-done(((f32[16,1,1,32]{3,2,1,0:T(1,128)}), f32[16,1,1,32]{3,2,1,0:T(1,128)S(1)}, u32[]{:S(2)}, u32[]{:S(2)}) %all-to-all-start.6) | async-done | bytes 2080 | tf_op jit(solution)/shard_map/all_to_all | solution.py:118
  173.5 3.5 %all-to-all-start.7 = ((f32[16,1,1,32]{3,2,1,0:T(1,128)}), f32[16,1,1,32]{3,2,1,0:T(1,128)S(1)}, u32[]{:S(2)}, u32[]{:S(2)}) async-start(f32[16,1,1,32]{3,2,1,0:T(1,128)} %copy.121), calls=%async_computation.7 | async-start | bytes 16384 | tf_op jit(solution)/shard_map/all_to_all | solution.py:117
  183.4 3.5 %all-to-all-start.9 = ((f32[16,1,1,32]{3,2,1,0:T(1,128)}), f32[16,1,1,32]{3,2,1,0:T(1,128)S(1)}, u32[]{:S(2)}, u32[]{:S(2)}) async-start(f32[16,1,1,32]{3,2,1,0:T(1,128)} %copy.127), calls=%async_computation.9 | async-start | bytes 16384 | tf_op jit(solution)/shard_map/all_to_all | solution.py:118
  193.2 3.5 %all-to-all-start.10 = ((f32[16,1,1,32]{3,2,1,0:T(1,128)}), f32[16,1,1,32]{3,2,1,0:T(1,128)S(1)}, u32[]{:S(2)}, u32[]{:S(2)}) async-start(f32[16,1,1,32]{3,2,1,0:T(1,128)} %copy.128), calls=%async_computation.10 | async-start | bytes 16384 | tf_op jit(solution)/shard_map/all_to_all | solution.py:117
  203.0 3.5 %all-to-all-start.2 = ((f32[16,1,1,4096]{3,1,2,0:T(1,128)}), f32[16,1,1,4096]{3,1,2,0:T(1,128)S(1)}, u32[]{:S(2)}, u32[]{:S(2)}) async-start(f32[16,1,1,4096]{3,1,2,0:T(1,128)} %bitcast.19), calls=%async_computation.2 | async-start | bytes 524288 | tf_op jit(solution)/shard_map/all_to_all | solution.py:116
  206.6 3.7 %fusion.55 = f32[16,1,4,8,128]{4,0,3,2,1:T(8,128)S(1)} fusion(bf16[1920,4,128,1]{0,2,3,1:T(8,128)(2,1)} %bitcast.351, f32[4,1920,16,8]{1,2,3,0:T(8,128)} %get-tuple-element.101, f32[16,4,8]{0,2,1:T(8,128)S(1)} %get-tuple-element.100, f32[16,4,8]{0,2,1:T(8,128)S(1)} %fusion.17), kind=kOutput, calls=%fused_computation.67 | convolution fusion | flops 254672896 | bytes 6164480 | tf_op jit(solution)/shard_map/while/body/eval_jaxpr/rtkgp,pkd->rtkgd/dot_general | solution.py:86
  212.8 3.7 %all-to-all-done.2 = f32[16,1,1,4096]{3,1,2,0:T(1,128)S(1)} async-done(((f32[16,1,1,4096]{3,1,2,0:T(1,128)}), f32[16,1,1,4096]{3,1,2,0:T(1,128)S(1)}, u32[]{:S(2)}, u32[]{:S(2)}) %all-to-all-start.2) | async-done | bytes 262176 | tf_op jit(solution)/shard_map/all_to_all | solution.py:116
  216.6 3.5 %all-to-all-start.5 = ((f32[16,1,1,4096]{3,1,2,0:T(1,128)}), f32[16,1,1,4096]{3,1,2,0:T(1,128)S(1)}, u32[]{:S(2)}, u32[]{:S(2)}) async-start(f32[16,1,1,4096]{3,1,2,0:T(1,128)} %bitcast.35), calls=%async_computation.5 | async-start | bytes 524288 | tf_op jit(solution)/shard_map/all_to_all | solution.py:116
  220.2 10.0 %all-to-all-done.5 = f32[16,1,1,4096]{3,1,2,0:T(1,128)S(1)} async-done(((f32[16,1,1,4096]{3,1,2,0:T(1,128)}), f32[16,1,1,4096]{3,1,2,0:T(1,128)S(1)}, u32[]{:S(2)}, u32[]{:S(2)}) %all-to-all-start.5) | async-done | bytes 262176 | tf_op jit(solution)/shard_map/all_to_all | solution.py:116
  230.1 3.5 %all-to-all-start.8 = ((f32[16,1,1,4096]{3,1,2,0:T(1,128)}), f32[16,1,1,4096]{3,1,2,0:T(1,128)S(1)}, u32[]{:S(2)}, u32[]{:S(2)}) async-start(f32[16,1,1,4096]{3,1,2,0:T(1,128)} %bitcast.50), calls=%async_computation.8 | async-start | bytes 524288 | tf_op jit(solution)/shard_map/all_to_all | solution.py:116
  233.7 9.9 %all-to-all-done.8 = f32[16,1,1,4096]{3,1,2,0:T(1,128)S(1)} async-done(((f32[16,1,1,4096]{3,1,2,0:T(1,128)}), f32[16,1,1,4096]{3,1,2,0:T(1,128)S(1)}, u32[]{:S(2)}, u32[]{:S(2)}) %all-to-all-start.8) | async-done | bytes 262176 | tf_op jit(solution)/shard_map/all_to_all | solution.py:116
  243.7 3.5 %all-to-all-start.11 = ((f32[16,1,1,4096]{3,1,2,0:T(1,128)}), f32[16,1,1,4096]{3,1,2,0:T(1,128)S(1)}, u32[]{:S(2)}, u32[]{:S(2)}) async-start(f32[16,1,1,4096]{3,1,2,0:T(1,128)} %bitcast.65), calls=%async_computation.11 | async-start | bytes 524288 | tf_op jit(solution)/shard_map/all_to_all | solution.py:116
  248.5 8.7 %all-to-all-done.11 = f32[16,1,1,4096]{3,1,2,0:T(1,128)S(1)} async-done(((f32[16,1,1,4096]{3,1,2,0:T(1,128)}), f32[16,1,1,4096]{3,1,2,0:T(1,128)S(1)}, u32[]{:S(2)}, u32[]{:S(2)}) %all-to-all-start.11) | async-done | bytes 262176 | tf_op jit(solution)/shard_map/all_to_all | solution.py:116
  (237 shorter events, 106.9 us)
Async XLA Ops:
  2.7 9.6 %collective-permute-start = (bf16[1,1,4096]{2,0,1:T(2,128)(2,1)S(1)}, bf16[1,1,4096]{2,0,1:T(2,128)(2,1)S(1)}, u32[]{:S(2)}, u32[]{:S(2)}) collective-permute-start(bf16[1,1,4096]{2,0,1:T(2,128)(2,1)S(1)} %get-tuple-element.76), channel_id=1, source_target_pairs={{0,1},{1,2},{2,3},{3,4},{4,5},{5,6},{6,7},{7,8},{8,9},{9,10},{10,1... | collective-permute-start | bytes 24584 | tf_op jit(solution)/shard_map/ppermute | solution.py:104
  3.2 9.1 %collective-permute-start.15 = (bf16[1,1,4096]{2,0,1:T(2,128)(2,1)S(1)}, bf16[1,1,4096]{2,0,1:T(2,128)(2,1)S(1)}, u32[]{:S(2)}, u32[]{:S(2)}) collective-permute-start(bf16[1,1,4096]{2,0,1:T(2,128)(2,1)S(1)} %get-tuple-element.86), channel_id=1, source_target_pairs={{0,1},{1,2},{2,3},{3,4},{4,5},{5,6},{6,7},{7,8},{8,9},{9,10},{10,1... | collective-permute-start | bytes 24584 | tf_op jit(solution)/shard_map/ppermute | solution.py:104
  5.8 21.0 %collective-permute-start.30 = (bf16[1,1,4096]{2,0,1:T(2,128)(2,1)S(1)}, bf16[1,1,4096]{2,0,1:T(2,128)(2,1)S(1)}, u32[]{:S(2)}, u32[]{:S(2)}) collective-permute-start(bf16[1,1,4096]{2,0,1:T(2,128)(2,1)S(1)} %get-tuple-element.85), channel_id=1, source_target_pairs={{0,1},{1,2},{2,3},{3,4},{4,5},{5,6},{6,7},{7,8},{8,9},{9,10},{10,1... | collective-permute-start | bytes 24584 | tf_op jit(solution)/shard_map/ppermute | solution.py:104
  5.9 21.0 %collective-permute-start.45 = (bf16[1,1,4096]{2,0,1:T(2,128)(2,1)S(1)}, bf16[1,1,4096]{2,0,1:T(2,128)(2,1)S(1)}, u32[]{:S(2)}, u32[]{:S(2)}) collective-permute-start(bf16[1,1,4096]{2,0,1:T(2,128)(2,1)S(1)} %get-tuple-element.84), channel_id=1, source_target_pairs={{0,1},{1,2},{2,3},{3,4},{4,5},{5,6},{6,7},{7,8},{8,9},{9,10},{10,1... | collective-permute-start | bytes 24584 | tf_op jit(solution)/shard_map/ppermute | solution.py:104
  12.3 16.2 %collective-permute-start.1 = (bf16[1,1,4096]{2,0,1:T(2,128)(2,1)S(1)}, bf16[1,1,4096]{2,0,1:T(2,128)(2,1)S(1)}, u32[]{:S(2)}, u32[]{:S(2)}) collective-permute-start(bf16[1,1,4096]{2,0,1:T(2,128)(2,1)S(1)} %collective-permute-done), channel_id=1, source_target_pairs={{0,1},{1,2},{2,3},{3,4},{4,5},{5,6},{6,7},{7,8},{8,9},{9,10},{10,1... | collective-permute-start | bytes 24584 | tf_op jit(solution)/shard_map/ppermute | solution.py:104
  12.3 16.2 %collective-permute-start.16 = (bf16[1,1,4096]{2,0,1:T(2,128)(2,1)S(1)}, bf16[1,1,4096]{2,0,1:T(2,128)(2,1)S(1)}, u32[]{:S(2)}, u32[]{:S(2)}) collective-permute-start(bf16[1,1,4096]{2,0,1:T(2,128)(2,1)S(1)} %collective-permute-done.15), channel_id=1, source_target_pairs={{0,1},{1,2},{2,3},{3,4},{4,5},{5,6},{6,7},{7,8},{8,9},{9,10},{10,1... | collective-permute-start | bytes 24584 | tf_op jit(solution)/shard_map/ppermute | solution.py:104
  26.8 9.7 %collective-permute-start.31 = (bf16[1,1,4096]{2,0,1:T(2,128)(2,1)S(1)}, bf16[1,1,4096]{2,0,1:T(2,128)(2,1)S(1)}, u32[]{:S(2)}, u32[]{:S(2)}) collective-permute-start(bf16[1,1,4096]{2,0,1:T(2,128)(2,1)S(1)} %collective-permute-done.30), channel_id=1, source_target_pairs={{0,1},{1,2},{2,3},{3,4},{4,5},{5,6},{6,7},{7,8},{8,9},{9,10},{10,1... | collective-permute-start | bytes 24584 | tf_op jit(solution)/shard_map/ppermute | solution.py:104
  26.9 9.7 %collective-permute-start.46 = (bf16[1,1,4096]{2,0,1:T(2,128)(2,1)S(1)}, bf16[1,1,4096]{2,0,1:T(2,128)(2,1)S(1)}, u32[]{:S(2)}, u32[]{:S(2)}) collective-permute-start(bf16[1,1,4096]{2,0,1:T(2,128)(2,1)S(1)} %collective-permute-done.45), channel_id=1, source_target_pairs={{0,1},{1,2},{2,3},{3,4},{4,5},{5,6},{6,7},{7,8},{8,9},{9,10},{10,1... | collective-permute-start | bytes 24584 | tf_op jit(solution)/shard_map/ppermute | solution.py:104
  28.5 9.7 %collective-permute-start.2 = (bf16[1,1,4096]{2,0,1:T(2,128)(2,1)S(1)}, bf16[1,1,4096]{2,0,1:T(2,128)(2,1)S(1)}, u32[]{:S(2)}, u32[]{:S(2)}) collective-permute-start(bf16[1,1,4096]{2,0,1:T(2,128)(2,1)S(1)} %collective-permute-done.1), channel_id=1, source_target_pairs={{0,1},{1,2},{2,3},{3,4},{4,5},{5,6},{6,7},{7,8},{8,9},{9,10},{10,1... | collective-permute-start | bytes 24584 | tf_op jit(solution)/shard_map/ppermute | solution.py:104
  28.6 9.7 %collective-permute-start.17 = (bf16[1,1,4096]{2,0,1:T(2,128)(2,1)S(1)}, bf16[1,1,4096]{2,0,1:T(2,128)(2,1)S(1)}, u32[]{:S(2)}, u32[]{:S(2)}) collective-permute-start(bf16[1,1,4096]{2,0,1:T(2,128)(2,1)S(1)} %collective-permute-done.16), channel_id=1, source_target_pairs={{0,1},{1,2},{2,3},{3,4},{4,5},{5,6},{6,7},{7,8},{8,9},{9,10},{10,1... | collective-permute-start | bytes 24584 | tf_op jit(solution)/shard_map/ppermute | solution.py:104
  36.5 10.2 %collective-permute-start.32 = (bf16[1,1,4096]{2,0,1:T(2,128)(2,1)S(1)}, bf16[1,1,4096]{2,0,1:T(2,128)(2,1)S(1)}, u32[]{:S(2)}, u32[]{:S(2)}) collective-permute-start(bf16[1,1,4096]{2,0,1:T(2,128)(2,1)S(1)} %collective-permute-done.31), channel_id=1, source_target_pairs={{0,1},{1,2},{2,3},{3,4},{4,5},{5,6},{6,7},{7,8},{8,9},{9,10},{10,1... | collective-permute-start | bytes 24584 | tf_op jit(solution)/shard_map/ppermute | solution.py:104
  36.6 10.2 %collective-permute-start.47 = (bf16[1,1,4096]{2,0,1:T(2,128)(2,1)S(1)}, bf16[1,1,4096]{2,0,1:T(2,128)(2,1)S(1)}, u32[]{:S(2)}, u32[]{:S(2)}) collective-permute-start(bf16[1,1,4096]{2,0,1:T(2,128)(2,1)S(1)} %collective-permute-done.46), channel_id=1, source_target_pairs={{0,1},{1,2},{2,3},{3,4},{4,5},{5,6},{6,7},{7,8},{8,9},{9,10},{10,1... | collective-permute-start | bytes 24584 | tf_op jit(solution)/shard_map/ppermute | solution.py:104
  38.2 8.7 %collective-permute-start.3 = (bf16[1,1,4096]{2,0,1:T(2,128)(2,1)S(1)}, bf16[1,1,4096]{2,0,1:T(2,128)(2,1)S(1)}, u32[]{:S(2)}, u32[]{:S(2)}) collective-permute-start(bf16[1,1,4096]{2,0,1:T(2,128)(2,1)S(1)} %collective-permute-done.2), channel_id=1, source_target_pairs={{0,1},{1,2},{2,3},{3,4},{4,5},{5,6},{6,7},{7,8},{8,9},{9,10},{10,1... | collective-permute-start | bytes 24584 | tf_op jit(solution)/shard_map/ppermute | solution.py:104
  38.2 8.7 %collective-permute-start.18 = (bf16[1,1,4096]{2,0,1:T(2,128)(2,1)S(1)}, bf16[1,1,4096]{2,0,1:T(2,128)(2,1)S(1)}, u32[]{:S(2)}, u32[]{:S(2)}) collective-permute-start(bf16[1,1,4096]{2,0,1:T(2,128)(2,1)S(1)} %collective-permute-done.17), channel_id=1, source_target_pairs={{0,1},{1,2},{2,3},{3,4},{4,5},{5,6},{6,7},{7,8},{8,9},{9,10},{10,1... | collective-permute-start | bytes 24584 | tf_op jit(solution)/shard_map/ppermute | solution.py:104
  46.9 8.5 %collective-permute-start.4 = (bf16[1,1,4096]{2,0,1:T(2,128)(2,1)S(1)}, bf16[1,1,4096]{2,0,1:T(2,128)(2,1)S(1)}, u32[]{:S(2)}, u32[]{:S(2)}) collective-permute-start(bf16[1,1,4096]{2,0,1:T(2,128)(2,1)S(1)} %collective-permute-done.3), channel_id=1, source_target_pairs={{0,1},{1,2},{2,3},{3,4},{4,5},{5,6},{6,7},{7,8},{8,9},{9,10},{10,1... | collective-permute-start | bytes 24584 | tf_op jit(solution)/shard_map/ppermute | solution.py:104
  46.9 8.5 %collective-permute-start.19 = (bf16[1,1,4096]{2,0,1:T(2,128)(2,1)S(1)}, bf16[1,1,4096]{2,0,1:T(2,128)(2,1)S(1)}, u32[]{:S(2)}, u32[]{:S(2)}) collective-permute-start(bf16[1,1,4096]{2,0,1:T(2,128)(2,1)S(1)} %collective-permute-done.18), channel_id=1, source_target_pairs={{0,1},{1,2},{2,3},{3,4},{4,5},{5,6},{6,7},{7,8},{8,9},{9,10},{10,1... | collective-permute-start | bytes 24584 | tf_op jit(solution)/shard_map/ppermute | solution.py:104
  71.4 9.1 %collective-permute-start.37 = (bf16[1,1,4096]{2,0,1:T(2,128)(2,1)S(1)}, bf16[1,1,4096]{2,0,1:T(2,128)(2,1)S(1)}, u32[]{:S(2)}, u32[]{:S(2)}) collective-permute-start(bf16[1,1,4096]{2,0,1:T(2,128)(2,1)S(1)} %collective-permute-done.36), channel_id=1, source_target_pairs={{0,1},{1,2},{2,3},{3,4},{4,5},{5,6},{6,7},{7,8},{8,9},{9,10},{10,1... | collective-permute-start | bytes 24584 | tf_op jit(solution)/shard_map/ppermute | solution.py:104
  71.5 9.0 %collective-permute-start.52 = (bf16[1,1,4096]{2,0,1:T(2,128)(2,1)S(1)}, bf16[1,1,4096]{2,0,1:T(2,128)(2,1)S(1)}, u32[]{:S(2)}, u32[]{:S(2)}) collective-permute-start(bf16[1,1,4096]{2,0,1:T(2,128)(2,1)S(1)} %collective-permute-done.51), channel_id=1, source_target_pairs={{0,1},{1,2},{2,3},{3,4},{4,5},{5,6},{6,7},{7,8},{8,9},{9,10},{10,1... | collective-permute-start | bytes 24584 | tf_op jit(solution)/shard_map/ppermute | solution.py:104
  115.7 15.3 %collective-permute-start.44 = (bf16[1,1,4096]{2,0,1:T(2,128)(2,1)S(1)}, bf16[1,1,4096]{2,0,1:T(2,128)(2,1)S(1)}, u32[]{:S(2)}, u32[]{:S(2)}) collective-permute-start(bf16[1,1,4096]{2,0,1:T(2,128)(2,1)S(1)} %collective-permute-done.43), channel_id=1, source_target_pairs={{0,1},{1,2},{2,3},{3,4},{4,5},{5,6},{6,7},{7,8},{8,9},{9,10},{10,1... | collective-permute-start | bytes 24584 | tf_op jit(solution)/shard_map/ppermute | solution.py:104
  115.9 15.5 %collective-permute-start.59 = (bf16[1,1,4096]{2,0,1:T(2,128)(2,1)S(1)}, bf16[1,1,4096]{2,0,1:T(2,128)(2,1)S(1)}, u32[]{:S(2)}, u32[]{:S(2)}) collective-permute-start(bf16[1,1,4096]{2,0,1:T(2,128)(2,1)S(1)} %collective-permute-done.58), channel_id=1, source_target_pairs={{0,1},{1,2},{2,3},{3,4},{4,5},{5,6},{6,7},{7,8},{8,9},{9,10},{10,1... | collective-permute-start | bytes 24584 | tf_op jit(solution)/shard_map/ppermute | solution.py:104
  122.2 11.0 %all-to-all-start = ((f32[16,1,1,32]{3,2,1,0:T(1,128)}), f32[16,1,1,32]{3,2,1,0:T(1,128)S(1)}, u32[]{:S(2)}, u32[]{:S(2)}) async-start(f32[16,1,1,32]{3,2,1,0:T(1,128)} %copy.106), calls=%async_computation | async-start | bytes 16384 | tf_op jit(solution)/shard_map/all_to_all | solution.py:118
  133.1 11.1 %all-to-all-start.1 = ((f32[16,1,1,32]{3,2,1,0:T(1,128)}), f32[16,1,1,32]{3,2,1,0:T(1,128)S(1)}, u32[]{:S(2)}, u32[]{:S(2)}) async-start(f32[16,1,1,32]{3,2,1,0:T(1,128)} %copy.107), calls=%async_computation.1 | async-start | bytes 16384 | tf_op jit(solution)/shard_map/all_to_all | solution.py:117
  144.2 9.8 %all-to-all-start.3 = ((f32[16,1,1,32]{3,2,1,0:T(1,128)}), f32[16,1,1,32]{3,2,1,0:T(1,128)S(1)}, u32[]{:S(2)}, u32[]{:S(2)}) async-start(f32[16,1,1,32]{3,2,1,0:T(1,128)} %copy.113), calls=%async_computation.3 | async-start | bytes 16384 | tf_op jit(solution)/shard_map/all_to_all | solution.py:118
  154.0 9.8 %all-to-all-start.4 = ((f32[16,1,1,32]{3,2,1,0:T(1,128)}), f32[16,1,1,32]{3,2,1,0:T(1,128)S(1)}, u32[]{:S(2)}, u32[]{:S(2)}) async-start(f32[16,1,1,32]{3,2,1,0:T(1,128)} %copy.114), calls=%async_computation.4 | async-start | bytes 16384 | tf_op jit(solution)/shard_map/all_to_all | solution.py:117
  163.8 9.8 %all-to-all-start.6 = ((f32[16,1,1,32]{3,2,1,0:T(1,128)}), f32[16,1,1,32]{3,2,1,0:T(1,128)S(1)}, u32[]{:S(2)}, u32[]{:S(2)}) async-start(f32[16,1,1,32]{3,2,1,0:T(1,128)} %copy.120), calls=%async_computation.6 | async-start | bytes 16384 | tf_op jit(solution)/shard_map/all_to_all | solution.py:118
  173.5 9.9 %all-to-all-start.7 = ((f32[16,1,1,32]{3,2,1,0:T(1,128)}), f32[16,1,1,32]{3,2,1,0:T(1,128)S(1)}, u32[]{:S(2)}, u32[]{:S(2)}) async-start(f32[16,1,1,32]{3,2,1,0:T(1,128)} %copy.121), calls=%async_computation.7 | async-start | bytes 16384 | tf_op jit(solution)/shard_map/all_to_all | solution.py:117
  183.4 9.8 %all-to-all-start.9 = ((f32[16,1,1,32]{3,2,1,0:T(1,128)}), f32[16,1,1,32]{3,2,1,0:T(1,128)S(1)}, u32[]{:S(2)}, u32[]{:S(2)}) async-start(f32[16,1,1,32]{3,2,1,0:T(1,128)} %copy.127), calls=%async_computation.9 | async-start | bytes 16384 | tf_op jit(solution)/shard_map/all_to_all | solution.py:118
  193.2 9.9 %all-to-all-start.10 = ((f32[16,1,1,32]{3,2,1,0:T(1,128)}), f32[16,1,1,32]{3,2,1,0:T(1,128)S(1)}, u32[]{:S(2)}, u32[]{:S(2)}) async-start(f32[16,1,1,32]{3,2,1,0:T(1,128)} %copy.128), calls=%async_computation.10 | async-start | bytes 16384 | tf_op jit(solution)/shard_map/all_to_all | solution.py:117
  203.0 13.5 %all-to-all-start.2 = ((f32[16,1,1,4096]{3,1,2,0:T(1,128)}), f32[16,1,1,4096]{3,1,2,0:T(1,128)S(1)}, u32[]{:S(2)}, u32[]{:S(2)}) async-start(f32[16,1,1,4096]{3,1,2,0:T(1,128)} %bitcast.19), calls=%async_computation.2 | async-start | bytes 524288 | tf_op jit(solution)/shard_map/all_to_all | solution.py:116
  216.6 13.5 %all-to-all-start.5 = ((f32[16,1,1,4096]{3,1,2,0:T(1,128)}), f32[16,1,1,4096]{3,1,2,0:T(1,128)S(1)}, u32[]{:S(2)}, u32[]{:S(2)}) async-start(f32[16,1,1,4096]{3,1,2,0:T(1,128)} %bitcast.35), calls=%async_computation.5 | async-start | bytes 524288 | tf_op jit(solution)/shard_map/all_to_all | solution.py:116
  230.1 13.5 %all-to-all-start.8 = ((f32[16,1,1,4096]{3,1,2,0:T(1,128)}), f32[16,1,1,4096]{3,1,2,0:T(1,128)S(1)}, u32[]{:S(2)}, u32[]{:S(2)}) async-start(f32[16,1,1,4096]{3,1,2,0:T(1,128)} %bitcast.50), calls=%async_computation.8 | async-start | bytes 524288 | tf_op jit(solution)/shard_map/all_to_all | solution.py:116
  243.7 13.5 %all-to-all-start.11 = ((f32[16,1,1,4096]{3,1,2,0:T(1,128)}), f32[16,1,1,4096]{3,1,2,0:T(1,128)S(1)}, u32[]{:S(2)}, u32[]{:S(2)}) async-start(f32[16,1,1,4096]{3,1,2,0:T(1,128)} %bitcast.65), calls=%async_computation.11 | async-start | bytes 524288 | tf_op jit(solution)/shard_map/all_to_all | solution.py:116
  (54 other events, 396.5 us)
